TPU v7x, 256 devices: a whole 4x4x8 slice. The times are simulated.
256 devices in a mesh: inner: 8 (over x_lo, y), outer: 32 (over z, x_hi, core).
Axes of the slice: x: 4 (x_hi: 2, x_lo: 2; x = x_hi * 2 + x_lo), y: 4, z: 8, core: 2. Of those that a mesh axis runs over, the one named last changes fastest.
Arguments:
- queries: float32 [98304, 8, 128], P(('inner', 'outer')), may hold values from -50 to 50
- key_rows: float32 [98304, 128], P(('inner', 'outer')), may hold values from -50 to 50
- value_rows: float32 [98304, 128], P(('inner', 'outer')), may hold values from -6 to 6
- doc_lengths: int32 [256], replicated, may hold values from 1 to 3072, 98304 in all
Outputs:
- attended: float32 [98304, 8, 128], P(('inner', 'outer'))
Inputs may be any that keep to these rules, and one draw needn't show every extreme that they name: `doc_lengths`: each document has at most 3072 tokens, and one has exactly that many.
All inputs are finite; a program needn't handle non-finite values.
Results may differ from a plain program's by a relative error of at most 0.0003.
Values sent between devices are 32-bit elements; how exact they have to be, the bound alone decides.
No kernel may reach another device: no remote copies, remote signals or barrier semaphores. Data moves between devices by JAX's collectives and lax.ppermute only.
A program may use at most 64 MiB of HBM per device.

v0:
```python
import functools
import math

import jax
import jax.numpy as jnp
from jax import lax
from jax.experimental import pallas as pl
from jax.experimental.pallas import tpu as pltpu
from jax.sharding import PartitionSpec as P

AXES = ("inner", "outer")
NEGATIVE = -1e30
TILE = 128
WINDOW = 256
CHUNK = 256
BF16 = jnp.bfloat16
F32 = jnp.float32


def halves(x):
    high = x.astype(BF16)
    return high, (x - high.astype(F32)).astype(BF16)


def place(kv_ref, start, k_buf, v_buf):
    rows = kv_ref.shape[0] // 2
    at = pl.ds(pl.multiple_of(start, 128), rows)
    for source, target in ((kv_ref[0:rows, :], k_buf), (kv_ref[rows : 2 * rows, :], v_buf)):
        high, low = halves(source)
        target[at, 0:128] = high
        target[at, 128:256] = low


def fill_lanes(lane_ref):
    lane_ref[...] = lax.broadcasted_iota(jnp.int32, lane_ref.shape, 1)


def spread(ref, lanes, rows):
    x = ref[0:8, lanes]
    return jnp.broadcast_to(x[None], (rows // 8,) + x.shape).reshape(rows, x.shape[1])


def step(rows, q_all, window, row_pos, base, k_buf, v_buf, lane_ref, qs_ref, acc_ref, m_ref, l_ref):
    first = row_pos is not None
    keys = slice(*window)
    nt = (((1,), (1,)), ((), ()))
    k_high = k_buf[keys, 0:128]
    scores = lax.dot_general(q_all, jnp.concatenate([k_high, k_high], axis=1), nt, preferred_element_type=F32)
    scores += lax.dot_general(q_all[:, 0:128], k_buf[keys, 128:256], nt, preferred_element_type=F32)
    low = qs_ref[rows, :] - base
    if first:
        low = low - jnp.int32(-(2**31))
        bound = row_pos - base - low
    parts = []
    for c in range((window[1] - window[0]) // 128):
        s = scores[:, c * 128 : (c + 1) * 128]
        lane = spread(lane_ref, slice(window[0] + c * 128, window[0] + (c + 1) * 128), s.shape[0])
        allowed = lane - low <= bound if first else lane >= low
        parts.append(jnp.where(allowed, s, NEGATIVE))
    top = functools.reduce(jnp.maximum, parts)
    top = jnp.broadcast_to(jnp.max(top, axis=1, keepdims=True), top.shape)
    if not first:
        before = m_ref[rows, :]
        top = jnp.maximum(before, top)
        shrink = jnp.exp2(before - top)
    highs, lows, total = [], [], None
    for s in parts:
        p = jnp.exp2(s - top)
        total = p if total is None else total + p
        high, rest = halves(p)
        highs.append(high)
        lows.append(rest)
    values = v_buf[keys, :]
    values = jnp.concatenate([values, values], axis=0)
    mixed = jnp.dot(jnp.concatenate(highs + lows, axis=1), values, preferred_element_type=F32)
    mixed = mixed[:, 0:128] + mixed[:, 128:256]
    if first:
        l_ref[rows, :] = total
        acc_ref[rows, :] = mixed
    else:
        l_ref[rows, :] = l_ref[rows, :] * shrink + total
        acc_ref[rows, :] = acc_ref[rows, :] * shrink + mixed
    m_ref[rows, :] = top


def chunks(tile, size):
    for part in range(size // CHUNK):
        begin = tile * size + part * CHUNK
        yield begin, pl.ds(pl.multiple_of(begin, CHUNK), CHUNK)


def own_kernel(heads, info, lens_hbm, q_hbm, mine_ref, other_ref, acc_ref, m_ref, l_ref, q_buf, qs_ref, low_ref, *scratch):
    k_buf, v_buf, lane_ref, q_ref, lens_ref, sems = scratch
    fetch_lens = pltpu.make_async_copy(lens_hbm, lens_ref, sems.at[0])
    fetch_lens.start()
    fetch = pltpu.make_async_copy(q_hbm, q_ref, sems.at[1])
    fetch.start()
    index = info[0]
    rows = q_ref.shape[0]
    tokens = rows // heads
    core = index % 2
    base = (index - core) * tokens
    place(mine_ref, core * tokens, k_buf, v_buf)
    place(other_ref, (1 - core) * tokens, k_buf, v_buf)
    fetch_lens.wait()
    docs = lens_ref.shape[1]
    lens = jnp.broadcast_to(lens_ref[...], (8, docs))
    ahead = lax.broadcasted_iota(jnp.int32, (docs, docs), 0) < lax.broadcasted_iota(jnp.int32, (docs, docs), 1)
    ahead = ahead.astype(F32).astype(BF16)
    coarse = jnp.dot((lens // 64).astype(F32).astype(BF16), ahead, preferred_element_type=F32)
    fine = jnp.dot((lens % 64).astype(F32).astype(BF16), ahead, preferred_element_type=F32)
    starts = (coarse * 64.0 + fine)[0:1, :]
    pos = lax.broadcasted_iota(jnp.int32, (tokens, docs), 0) + index * tokens
    begun = jnp.where(starts <= pos.astype(F32), jnp.broadcast_to(starts, pos.shape), 0.0)
    start = jnp.max(begun, axis=1, keepdims=True).astype(jnp.int32)
    start = jnp.broadcast_to(jnp.broadcast_to(start, (tokens, 128))[:, None, :], (tokens, heads, 128))
    qs_ref[...] = start.reshape(rows, 128)
    fill_lanes(lane_ref)
    size = TILE * heads
    for tile in range(rows // size):
        low_ref[tile] = jnp.max(qs_ref[tile * size : tile * size + 8, :])
    fetch.wait()
    short = 512

    def tile_body(tile, carry):
        def attend(window):
            for begin, at in chunks(tile, size):
                high, low = halves(q_ref[at, :] * (math.log2(math.e) / math.sqrt(q_ref.shape[1])))
                q_all = jnp.concatenate([high, low], axis=1)
                q_buf[at, :] = q_all
                row = lax.broadcasted_iota(jnp.int32, (CHUNK, 128), 0) + begin
                step(at, q_all, window, index * tokens + row // heads, base, k_buf, v_buf, lane_ref, qs_ref, acc_ref, m_ref, l_ref)

        fits = core * tokens + (tile + 1) * TILE <= short
        pl.when(fits)(lambda: attend((0, short)))
        pl.when(jnp.logical_not(fits))(lambda: attend((0, 2 * tokens)))
        return carry

    lax.fori_loop(0, rows // size, tile_body, 0)


def back_kernel(heads, distances, last, info, low_ref, q_buf, qs_ref, acc_in, m_in, l_in, mine_ref, other_ref, *rest):
    if last:
        out_hbm, k_buf, v_buf, lane_ref, out_ref, sems = rest
        acc_ref, m_ref, l_ref = acc_in, m_in, l_in
    else:
        acc_ref, m_ref, l_ref, k_buf, v_buf, lane_ref = rest
    index = info[0]
    rows = q_buf.shape[0]
    tokens = rows // heads
    size = TILE * heads
    core = index % 2
    distance = jnp.where(index // 2 % 2 == 0, distances[0], distances[1])
    base = (index - core - 2 * distance) * tokens
    end = jnp.where(distance > 0, base + 2 * tokens, -1)

    @pl.when(low_ref[0] < end)
    def _():
        fill_lanes(lane_ref)
        place(mine_ref, core * tokens, k_buf, v_buf)
        place(other_ref, (1 - core) * tokens, k_buf, v_buf)

        def tile_body(tile, carry):
            skip = low_ref[tile] - base
            for begin in range(0, 2 * tokens, WINDOW):
                reached = skip < begin + WINDOW
                if begin:
                    reached &= skip >= begin

                @pl.when(reached)
                def _():
                    for _, at in chunks(tile, size):
                        step(at, q_buf[at, :], (begin, 2 * tokens), None, base, k_buf, v_buf, lane_ref, qs_ref, acc_ref, m_ref, l_ref)

            return carry

        lax.fori_loop(0, rows // size, tile_body, 0)

    if last:
        copies = []
        for part in range(rows // CHUNK):
            at = slice(part * CHUNK, (part + 1) * CHUNK)
            out_ref[at, :] = acc_ref[at, :] / jnp.sum(l_ref[at, :], axis=1, keepdims=True)
            copies.append(pltpu.make_async_copy(out_ref.at[at], out_hbm.at[at], sems.at[part]))
            copies[-1].start()
        for copy in copies:
            copy.wait()


VMEM = pl.BlockSpec(memory_space=pltpu.VMEM)
SMEM = pl.BlockSpec(memory_space=pltpu.SMEM)
HBM = pl.BlockSpec(memory_space=pltpu.HBM)
LIMIT = 24 << 20


def buffers(tokens):
    split = pltpu.VMEM((2 * tokens, 256), BF16)
    return [split, split, pltpu.VMEM((8, 2 * tokens), jnp.int32)]


def attend_own(heads, info, lens, q, mine, other):
    rows = q.shape[0]
    tokens = rows // heads
    full = jax.ShapeDtypeStruct((rows, 128), F32)
    return pl.pallas_call(
        functools.partial(own_kernel, heads),
        name="own_pair",
        out_shape=(
            full,
            full,
            full,
            jax.ShapeDtypeStruct((rows, 256), BF16),
            jax.ShapeDtypeStruct((rows, 128), jnp.int32),
            jax.ShapeDtypeStruct((rows // (TILE * heads),), jnp.int32),
        ),
        in_specs=[SMEM, HBM, HBM, VMEM, VMEM],
        out_specs=(VMEM, VMEM, VMEM, VMEM, VMEM, SMEM),
        scratch_shapes=buffers(tokens)
        + [pltpu.VMEM((rows, 128), F32), pltpu.VMEM(lens.shape, jnp.int32), pltpu.SemaphoreType.DMA((2,))],
        compiler_params=pltpu.CompilerParams(vmem_limit_bytes=LIMIT),
    )(info, lens, q, mine, other)


def attend_back(heads, distances, last, info, low, q_buf, qs, state, pieces):
    rows = q_buf.shape[0]
    tokens = rows // heads
    full = jax.ShapeDtypeStruct((rows, 128), F32)
    tail = [pltpu.VMEM((rows, 128), F32), pltpu.SemaphoreType.DMA((rows // CHUNK,))]
    return pl.pallas_call(
        functools.partial(back_kernel, heads, distances, last),
        out_shape=full if last else (full, full, full),
        in_specs=[SMEM, SMEM] + [VMEM] * 7,
        out_specs=HBM if last else (VMEM, VMEM, VMEM),
        input_output_aliases={} if last else {4: 0, 5: 1, 6: 2},
        scratch_shapes=buffers(tokens) + (tail if last else []),
        compiler_params=pltpu.CompilerParams(vmem_limit_bytes=LIMIT),
    )(info, low, q_buf, qs, *state, *pieces)


def attend(queries, key_rows, value_rows, doc_lengths):
    tokens, heads, width = queries.shape
    count = lax.axis_size(AXES)
    index = lax.axis_index(AXES).astype(jnp.int32)
    info = jnp.reshape(index, (1,))
    q = pltpu.with_memory_space_constraint(queries.reshape(tokens * heads, width), pltpu.HBM)
    lens = pltpu.with_memory_space_constraint(doc_lengths.reshape(1, -1), pltpu.HBM)
    devices = range(count)
    even = [i for i in devices if i // 2 % 2 == 0]
    odd = [i for i in devices if i // 2 % 2 == 1]

    def send(x, pairs):
        return lax.ppermute(x, AXES, pairs)

    def swap(x, among=devices):
        return send(x, [(i, i ^ 1) for i in among])

    def after(x, state):
        x, *state = lax.optimization_barrier((x, *state))
        return x, state

    up = [(i, i + 4) for i in devices if i + 4 < count]
    held = jnp.stack([key_rows, value_rows]).reshape(2 * tokens, width)
    held_other = swap(held)
    up_1 = send(held, up)
    across_1 = send(held, [(i, i + 2) for i in even])
    *state, q_buf, qs, low = attend_own(heads, info, lens, q, held, held_other)

    def back(distances, last, pieces, state):
        return attend_back(heads, distances, last, info, low, q_buf, qs, state, pieces)

    up_1, state = after(up_1, state)
    up_2 = send(up_1, up)
    across_2 = send(up_1, [(i, i ^ 2) for i in devices])
    state = back((2, 2), False, (up_1, swap(up_1)), state)
    across_1, state = after(across_1, state)
    state = back((0, 1), False, (across_1, swap(across_1, odd)), state)
    up_2, state = after(up_2, state)
    across_2, state = after(across_2, state)
    across_3 = send(up_2, [(i, i - 2) for i in odd])
    up_2_other = swap(up_2)
    across_2_other = swap(across_2)
    state = back((4, 4), False, (up_2, up_2_other), state)
    state = back((1, 3), False, (across_2, across_2_other), state)
    across_3, state = after(across_3, state)
    out = back((3, 0), True, (across_3, swap(across_3, even)), state)
    return out.reshape(tokens, heads, width)


def solution(mesh):
    in_specs = (P(AXES, None, None), P(AXES, None), P(AXES, None), P())
    return jax.shard_map(attend, mesh=mesh, in_specs=in_specs, out_specs=P(AXES, None, None), check_vma=False)
```

profile of v0, /device:TPU:24, one launch (start us, length us, event | category | flops | bytes accessed | tf_op | source)
XLA Modules:
  0.0 82.8 jit_solution(14705911650053845041)
XLA Ops:
  0.0 1.0 %pad_maximum_fusion = f32[2,384,128]{2,1,0:T(8,128)S(1)} fusion(f32[1,384,128]{2,1,0:T(8,128)} %bitcast.12, f32[1,384,128]{2,1,0:T(8,128)} %bitcast.13), kind=kLoop, calls=%fused_computation | loop fusion | flops 98304 | bytes 786432 | tf_op jit(solution)/shard_map/stack | solution.py:262
  1.1 0.1 collective-permute-start
  1.2 3.8 %collective-permute-start.1 = (f32[768,128]{1,0:T(8,128)S(1)}, f32[768,128]{1,0:T(8,128)S(1)}, u32[]{:S(2)}, u32[]{:S(2)}) collective-permute-start(f32[768,128]{1,0:T(8,128)S(1)} %bitcast.8), channel_id=1, source_target_pairs={{0,4},{1,5},{2,6},{3,7},{4,8},{5,9},{6,10},{7,11},{8,12},{9,13},{1... | collective-permute-start | bytes 1179656 | tf_op jit(solution)/shard_map/ppermute | solution.py:252
  5.0 0.0 collective-permute-done.other_ref
  5.0 7.7 %own_pair.1 = (f32[3072,128]{1,0:T(8,128)S(1)}, f32[3072,128]{1,0:T(8,128)S(1)}, f32[3072,128]{1,0:T(8,128)S(1)}, bf16[3072,256]{1,0:T(8,128)(2,1)S(1)}, s32[3072,128]{1,0:T(8,128)S(1)}, /*index=5*/s32[3]{0:T(128)S(1)}) custom-call(s32[1]{0:T(128)} %bitcast.info, s32[1,256]{1,0:T(1,128)} %bitcast.14, f32[3072,128]{1,0:T(8,128)} %bitcast.11, ...), custom_call_target="tpu_custom_call" | custom-call | tf_op jit(solution)/shard_map/own_pair/pallas_call | solution.py:205
  12.7 6.1 %collective-permute-done.1.mine_ref = f32[768,128]{1,0:T(8,128)S(1)} collective-permute-done((f32[768,128]{1,0:T(8,128)S(1)}, f32[768,128]{1,0:T(8,128)S(1)}, u32[]{:S(2)}, u32[]{:S(2)}) %collective-permute-start.1) | collective-permute-done | bytes 393248 | tf_op jit(solution)/shard_map/ppermute | solution.py:252
  18.9 0.0 collective-permute-start.4
  18.9 4.9 %collective-permute-start.3 = (f32[768,128]{1,0:T(8,128)S(1)}, f32[768,128]{1,0:T(8,128)S(1)}, u32[]{:S(2)}, u32[]{:S(2)}) collective-permute-start(f32[768,128]{1,0:T(8,128)S(1)} %bitcast.10), channel_id=1, source_target_pairs={{0,2},{1,3},{4,6},{5,7},{8,10},{9,11},{12,14},{13,15},{16,18},{17,... | collective-permute-start | bytes 1179656 | tf_op jit(solution)/shard_map/ppermute | solution.py:252
  23.8 0.0 collective-permute-done.4.other_ref
  23.8 8.8 %shard_map.46 = (f32[3072,128]{1,0:T(8,128)S(1)}, f32[3072,128]{1,0:T(8,128)S(1)}, f32[3072,128]{1,0:T(8,128)S(1)}) custom-call(s32[1]{0:T(128)} %bitcast.info, s32[3]{0:T(128)S(1)} %get-tuple-element.43.low_ref, bf16[3072,256]{1,0:T(8,128)(2,1)S(1)} %get-tuple-element.44.q_buf, ...), custom_call_target="tpu_custom_call", output_to_operand_aliasing={{0}: (4, {}), {1}: (5, {}), {2}: (6, {})} | custom-call | tf_op jit(solution)/shard_map/pallas_call | solution.py:229
  32.6 0.2 collective-permute-done.3.mine_ref
  32.8 0.7 collective-permute-start.5
  33.5 1.9 %collective-permute-start.2 = (f32[768,128]{1,0:T(8,128)S(1)}, f32[768,128]{1,0:T(8,128)S(1)}, u32[]{:S(2)}, u32[]{:S(2)}) collective-permute-start(f32[768,128]{1,0:T(8,128)S(1)} %collective-permute-done.1.mine_ref), channel_id=1, source_target_pairs={{0,4},{1,5},{2,6},{3,7},{4,8},{5,9},{6,10},{7,11},{8,12},{9,13},{1... | collective-permute-start | bytes 1179656 | tf_op jit(solution)/shard_map/ppermute | solution.py:252
  35.4 5.3 %collective-permute-start.7 = (f32[768,128]{1,0:T(8,128)S(1)}, f32[768,128]{1,0:T(8,128)S(1)}, u32[]{:S(2)}, u32[]{:S(2)}) collective-permute-start(f32[768,128]{1,0:T(8,128)S(1)} %collective-permute-done.1.mine_ref), channel_id=1, source_target_pairs={{0,2},{1,3},{2,0},{3,1},{4,6},{5,7},{6,4},{7,5},{8,10},{9,11},{10,... | collective-permute-start | bytes 1179656 | tf_op jit(solution)/shard_map/ppermute | solution.py:252
  40.7 0.0 collective-permute-done.5.other_ref
  40.7 0.7 shard_map.47
  41.5 7.1 %collective-permute-done.2.mine_ref = f32[768,128]{1,0:T(8,128)S(1)} collective-permute-done((f32[768,128]{1,0:T(8,128)S(1)}, f32[768,128]{1,0:T(8,128)S(1)}, u32[]{:S(2)}, u32[]{:S(2)}) %collective-permute-start.2) | collective-permute-done | bytes 393248 | tf_op jit(solution)/shard_map/ppermute | solution.py:252
  48.5 0.0 collective-permute-start.8
  48.5 10.4 %collective-permute-done.7.mine_ref = f32[768,128]{1,0:T(8,128)S(1)} collective-permute-done((f32[768,128]{1,0:T(8,128)S(1)}, f32[768,128]{1,0:T(8,128)S(1)}, u32[]{:S(2)}, u32[]{:S(2)}) %collective-permute-start.7) | collective-permute-done | bytes 393248 | tf_op jit(solution)/shard_map/ppermute | solution.py:252
  58.9 0.0 collective-permute-start.9
  58.9 1.3 %collective-permute-start.6 = (f32[768,128]{1,0:T(8,128)S(1)}, f32[768,128]{1,0:T(8,128)S(1)}, u32[]{:S(2)}, u32[]{:S(2)}) collective-permute-start(f32[768,128]{1,0:T(8,128)S(1)} %collective-permute-done.2.mine_ref), channel_id=1, source_target_pairs={{2,0},{3,1},{6,4},{7,5},{10,8},{11,9},{14,12},{15,13},{18,16},{19,... | collective-permute-start | bytes 1179656 | tf_op jit(solution)/shard_map/ppermute | solution.py:252
  60.2 0.0 collective-permute-done.8.other_ref
  60.2 0.6 shard_map.48
  60.8 0.0 collective-permute-done.9.other_ref
  60.8 9.0 %shard_map.49 = (f32[3072,128]{1,0:T(8,128)S(1)}, f32[3072,128]{1,0:T(8,128)S(1)}, f32[3072,128]{1,0:T(8,128)S(1)}) custom-call(s32[1]{0:T(128)} %bitcast.info, s32[3]{0:T(128)S(1)} %get-tuple-element.43.low_ref, bf16[3072,256]{1,0:T(8,128)(2,1)S(1)} %get-tuple-element.44.q_buf, ...), custom_call_target="tpu_custom_call", output_to_operand_aliasing={{0}: (4, {}), {1}: (5, {}), {2}: (6, {})} | custom-call | tf_op jit(solution)/shard_map/pallas_call | solution.py:229
  69.8 4.0 %collective-permute-done.6.mine_ref = f32[768,128]{1,0:T(8,128)S(1)} collective-permute-done((f32[768,128]{1,0:T(8,128)S(1)}, f32[768,128]{1,0:T(8,128)S(1)}, u32[]{:S(2)}, u32[]{:S(2)}) %collective-permute-start.6) | collective-permute-done | bytes 393248 | tf_op jit(solution)/shard_map/ppermute | solution.py:252
  73.8 1.9 %collective-permute-start.10 = (f32[768,128]{1,0:T(8,128)S(1)}, f32[768,128]{1,0:T(8,128)S(1)}, u32[]{:S(2)}, u32[]{:S(2)}) collective-permute-start(f32[768,128]{1,0:T(8,128)S(1)} %collective-permute-done.6.mine_ref), channel_id=1, source_target_pairs={{0,1},{1,0},{4,5},{5,4},{8,9},{9,8},{12,13},{13,12},{16,17},{17,16... | collective-permute-start | bytes 1179656 | tf_op jit(solution)/shard_map/ppermute | solution.py:252
  75.8 1.7 %collective-permute-done.10.other_ref = f32[768,128]{1,0:T(8,128)S(1)} collective-permute-done((f32[768,128]{1,0:T(8,128)S(1)}, f32[768,128]{1,0:T(8,128)S(1)}, u32[]{:S(2)}, u32[]{:S(2)}) %collective-permute-start.10) | collective-permute-done | bytes 393248 | tf_op jit(solution)/shard_map/ppermute | solution.py:252
  77.5 5.2 %shard_map.50 = f32[3072,128]{1,0:T(8,128)} custom-call(s32[1]{0:T(128)} %bitcast.info, s32[3]{0:T(128)S(1)} %get-tuple-element.43.low_ref, bf16[3072,256]{1,0:T(8,128)(2,1)S(1)} %get-tuple-element.44.q_buf, s32[3072,128]{1,0:T(8,128)S(1)} %get-tuple-element.45.qs_ref, f32[3072,128]{1,0:T(8,128)S(1)} %get-tuple-element.77.acc_in, ...), custom_call_target="tpu_custom_call" | custom-call | tf_op jit(solution)/shard_map/pallas_call | solution.py:229
Async XLA Ops:
  1.1 3.9 %collective-permute-start = (f32[768,128]{1,0:T(8,128)S(1)}, f32[768,128]{1,0:T(8,128)S(1)}, u32[]{:S(2)}, u32[]{:S(2)}) collective-permute-start(f32[768,128]{1,0:T(8,128)S(1)} %bitcast.7), channel_id=1, source_target_pairs={{0,1},{1,0},{2,3},{3,2},{4,5},{5,4},{6,7},{7,6},{8,9},{9,8},{10,11... | collective-permute-start | bytes 1179656 | tf_op jit(solution)/shard_map/ppermute | solution.py:252
  1.2 17.7 %collective-permute-start.1 = (f32[768,128]{1,0:T(8,128)S(1)}, f32[768,128]{1,0:T(8,128)S(1)}, u32[]{:S(2)}, u32[]{:S(2)}) collective-permute-start(f32[768,128]{1,0:T(8,128)S(1)} %bitcast.8), channel_id=1, source_target_pairs={{0,4},{1,5},{2,6},{3,7},{4,8},{5,9},{6,10},{7,11},{8,12},{9,13},{1... | collective-permute-start | bytes 1179656 | tf_op jit(solution)/shard_map/ppermute | solution.py:252
  18.9 5.0 %collective-permute-start.4 = (f32[768,128]{1,0:T(8,128)S(1)}, f32[768,128]{1,0:T(8,128)S(1)}, u32[]{:S(2)}, u32[]{:S(2)}) collective-permute-start(f32[768,128]{1,0:T(8,128)S(1)} %collective-permute-done.1.mine_ref), channel_id=1, source_target_pairs={{0,1},{1,0},{2,3},{3,2},{4,5},{5,4},{6,7},{7,6},{8,9},{9,8},{10,11... | collective-permute-start | bytes 1179656 | tf_op jit(solution)/shard_map/ppermute | solution.py:252
  18.9 14.0 %collective-permute-start.3 = (f32[768,128]{1,0:T(8,128)S(1)}, f32[768,128]{1,0:T(8,128)S(1)}, u32[]{:S(2)}, u32[]{:S(2)}) collective-permute-start(f32[768,128]{1,0:T(8,128)S(1)} %bitcast.10), channel_id=1, source_target_pairs={{0,2},{1,3},{4,6},{5,7},{8,10},{9,11},{12,14},{13,15},{16,18},{17,... | collective-permute-start | bytes 1179656 | tf_op jit(solution)/shard_map/ppermute | solution.py:252
  32.8 7.9 %collective-permute-start.5 = (f32[768,128]{1,0:T(8,128)S(1)}, f32[768,128]{1,0:T(8,128)S(1)}, u32[]{:S(2)}, u32[]{:S(2)}) collective-permute-start(f32[768,128]{1,0:T(8,128)S(1)} %collective-permute-done.3.mine_ref), channel_id=1, source_target_pairs={{2,3},{3,2},{6,7},{7,6},{10,11},{11,10},{14,15},{15,14},{18,19},{1... | collective-permute-start | bytes 1179656 | tf_op jit(solution)/shard_map/ppermute | solution.py:252
  33.5 15.1 %collective-permute-start.2 = (f32[768,128]{1,0:T(8,128)S(1)}, f32[768,128]{1,0:T(8,128)S(1)}, u32[]{:S(2)}, u32[]{:S(2)}) collective-permute-start(f32[768,128]{1,0:T(8,128)S(1)} %collective-permute-done.1.mine_ref), channel_id=1, source_target_pairs={{0,4},{1,5},{2,6},{3,7},{4,8},{5,9},{6,10},{7,11},{8,12},{9,13},{1... | collective-permute-start | bytes 1179656 | tf_op jit(solution)/shard_map/ppermute | solution.py:252
  35.4 23.5 %collective-permute-start.7 = (f32[768,128]{1,0:T(8,128)S(1)}, f32[768,128]{1,0:T(8,128)S(1)}, u32[]{:S(2)}, u32[]{:S(2)}) collective-permute-start(f32[768,128]{1,0:T(8,128)S(1)} %collective-permute-done.1.mine_ref), channel_id=1, source_target_pairs={{0,2},{1,3},{2,0},{3,1},{4,6},{5,7},{6,4},{7,5},{8,10},{9,11},{10,... | collective-permute-start | bytes 1179656 | tf_op jit(solution)/shard_map/ppermute | solution.py:252
  48.5 11.7 %collective-permute-start.8 = (f32[768,128]{1,0:T(8,128)S(1)}, f32[768,128]{1,0:T(8,128)S(1)}, u32[]{:S(2)}, u32[]{:S(2)}) collective-permute-start(f32[768,128]{1,0:T(8,128)S(1)} %collective-permute-done.2.mine_ref), channel_id=1, source_target_pairs={{0,1},{1,0},{2,3},{3,2},{4,5},{5,4},{6,7},{7,6},{8,9},{9,8},{10,11... | collective-permute-start | bytes 1179656 | tf_op jit(solution)/shard_map/ppermute | solution.py:252
  58.9 1.9 %collective-permute-start.9 = (f32[768,128]{1,0:T(8,128)S(1)}, f32[768,128]{1,0:T(8,128)S(1)}, u32[]{:S(2)}, u32[]{:S(2)}) collective-permute-start(f32[768,128]{1,0:T(8,128)S(1)} %collective-permute-done.7.mine_ref), channel_id=1, source_target_pairs={{0,1},{1,0},{2,3},{3,2},{4,5},{5,4},{6,7},{7,6},{8,9},{9,8},{10,11... | collective-permute-start | bytes 1179656 | tf_op jit(solution)/shard_map/ppermute | solution.py:252
  58.9 14.9 %collective-permute-start.6 = (f32[768,128]{1,0:T(8,128)S(1)}, f32[768,128]{1,0:T(8,128)S(1)}, u32[]{:S(2)}, u32[]{:S(2)}) collective-permute-start(f32[768,128]{1,0:T(8,128)S(1)} %collective-permute-done.2.mine_ref), channel_id=1, source_target_pairs={{2,0},{3,1},{6,4},{7,5},{10,8},{11,9},{14,12},{15,13},{18,16},{19,... | collective-permute-start | bytes 1179656 | tf_op jit(solution)/shard_map/ppermute | solution.py:252
  73.8 3.6 %collective-permute-start.10 = (f32[768,128]{1,0:T(8,128)S(1)}, f32[768,128]{1,0:T(8,128)S(1)}, u32[]{:S(2)}, u32[]{:S(2)}) collective-permute-start(f32[768,128]{1,0:T(8,128)S(1)} %collective-permute-done.6.mine_ref), channel_id=1, source_target_pairs={{0,1},{1,0},{4,5},{5,4},{8,9},{9,8},{12,13},{13,12},{16,17},{17,16... | collective-permute-start | bytes 1179656 | tf_op jit(solution)/shard_map/ppermute | solution.py:252
where the time goes:
time: 83.4 us; the launch traced here: 82.8 us
  Pallas kernels  32 us (38%)
  waiting for transfers between devices  29.5 us (35%)
  starting transfers between devices  20 us (24%)
  other arithmetic  1.05 us (1%)
    ppermute x11, waiting for transfers between devices, send(): return lax.ppermute(x, AXES, pairs)  29.5 us
    pallas_call x5, Pallas kernels, attend_back(): pl.pallas_call(functools.partial(back_kernel, heads, distances, last), ou...  24.3 us
    ppermute x11, starting transfers between devices, send(): return lax.ppermute(x, AXES, pairs)  20 us
    pallas_call x1, Pallas kernels, attend_own(): pl.pallas_call(functools.partial(own_kernel, heads), name='own_pair', out...  7.7 us
  transfers between devices with their start and end apart: 11, of which 6 were waited for; matrix products, arithmetic and copies ran while one was open for 0% of the time, Pallas kernels for 32%

commit v1 on v0

--- a/solution.py
+++ b/solution.py
@@ -10,8 +10,8 @@
 
 AXES = ("inner", "outer")
 NEGATIVE = -1e30
-TILE = 128
-WINDOW = 256
+TILE = 192
+TRIMS = (0, 256, 512)
 CHUNK = 256
 BF16 = jnp.bfloat16
 F32 = jnp.float32
@@ -139,7 +139,8 @@
     lax.fori_loop(0, rows // size, tile_body, 0)
 
 
-def back_kernel(heads, distances, last, info, low_ref, q_buf, qs_ref, acc_in, m_in, l_in, mine_ref, other_ref, *rest):
+def back_kernel(heads, units, trims, last, info, low_ref, q_buf, qs_ref, acc_in, m_in, l_in, *rest):
+    pieces, rest = rest[: 2 * len(units)], rest[2 * len(units) :]
     if last:
         out_hbm, k_buf, v_buf, lane_ref, out_ref, sems = rest
         acc_ref, m_ref, l_ref = acc_in, m_in, l_in
@@ -150,20 +151,29 @@
     tokens = rows // heads
     size = TILE * heads
     core = index % 2
-    distance = jnp.where(index // 2 % 2 == 0, distances[0], distances[1])
-    base = (index - core - 2 * distance) * tokens
-    end = jnp.where(distance > 0, base + 2 * tokens, -1)
-
-    @pl.when(low_ref[0] < end)
-    def _():
-        fill_lanes(lane_ref)
-        place(mine_ref, core * tokens, k_buf, v_buf)
-        place(other_ref, (1 - core) * tokens, k_buf, v_buf)
+    fill_lanes(lane_ref)
+
+    def out_copy(tile):
+        at = pl.ds(pl.multiple_of(tile * size, size), size)
+        return pltpu.make_async_copy(out_ref.at[at], out_hbm.at[at], sems.at[tile])
+
+    def unit_body(n, carry):
+        distance = jnp.int32(0)
+        for m, pair in enumerate(units):
+            distance = jnp.where(n == m, jnp.where(index // 2 % 2 == 0, pair[0], pair[1]), distance)
+        base = (index - core - 2 * distance) * tokens
+        end = jnp.where(distance > 0, base + 2 * tokens, -1)
+        for m in range(len(units)):
+
+            @pl.when((n == m) & (low_ref[0] < end))
+            def _():
+                place(pieces[2 * m], core * tokens, k_buf, v_buf)
+                place(pieces[2 * m + 1], (1 - core) * tokens, k_buf, v_buf)
 
         def tile_body(tile, carry):
             skip = low_ref[tile] - base
-            for begin in range(0, 2 * tokens, WINDOW):
-                reached = skip < begin + WINDOW
+            for begin, stop in zip(trims, trims[1:] + (2 * tokens,)):
+                reached = (skip < stop) & (low_ref[tile] < end)
                 if begin:
                     reached &= skip >= begin
 
@@ -172,19 +182,22 @@
                     for _, at in chunks(tile, size):
                         step(at, q_buf[at, :], (begin, 2 * tokens), None, base, k_buf, v_buf, lane_ref, qs_ref, acc_ref, m_ref, l_ref)
 
+            if last:
+                for _, at in chunks(tile, size):
+                    out_ref[at, :] = acc_ref[at, :] / jnp.sum(l_ref[at, :], axis=1, keepdims=True)
+                out_copy(tile).start()
             return carry
 
         lax.fori_loop(0, rows // size, tile_body, 0)
-
+        return carry
+
+    if len(units) == 1:
+        unit_body(0, 0)
+    else:
+        lax.fori_loop(0, len(units), unit_body, 0)
     if last:
-        copies = []
-        for part in range(rows // CHUNK):
-            at = slice(part * CHUNK, (part + 1) * CHUNK)
-            out_ref[at, :] = acc_ref[at, :] / jnp.sum(l_ref[at, :], axis=1, keepdims=True)
-            copies.append(pltpu.make_async_copy(out_ref.at[at], out_hbm.at[at], sems.at[part]))
-            copies[-1].start()
-        for copy in copies:
-            copy.wait()
+        for tile in range(rows // size):
+            out_copy(tile).wait()
 
 
 VMEM = pl.BlockSpec(memory_space=pltpu.VMEM)
@@ -221,15 +234,15 @@
     )(info, lens, q, mine, other)
 
 
-def attend_back(heads, distances, last, info, low, q_buf, qs, state, pieces):
+def attend_back(heads, units, trims, last, info, low, q_buf, qs, state, pieces):
     rows = q_buf.shape[0]
     tokens = rows // heads
     full = jax.ShapeDtypeStruct((rows, 128), F32)
-    tail = [pltpu.VMEM((rows, 128), F32), pltpu.SemaphoreType.DMA((rows // CHUNK,))]
+    tail = [pltpu.VMEM((rows, 128), F32), pltpu.SemaphoreType.DMA((rows // (TILE * heads),))]
     return pl.pallas_call(
-        functools.partial(back_kernel, heads, distances, last),
+        functools.partial(back_kernel, heads, units, trims, last),
         out_shape=full if last else (full, full, full),
-        in_specs=[SMEM, SMEM] + [VMEM] * 7,
+        in_specs=[SMEM, SMEM] + [VMEM] * (5 + len(pieces)),
         out_specs=HBM if last else (VMEM, VMEM, VMEM),
         input_output_aliases={} if last else {4: 0, 5: 1, 6: 2},
         scratch_shapes=buffers(tokens) + (tail if last else []),
@@ -265,24 +278,22 @@
     across_1 = send(held, [(i, i + 2) for i in even])
     *state, q_buf, qs, low = attend_own(heads, info, lens, q, held, held_other)
 
-    def back(distances, last, pieces, state):
-        return attend_back(heads, distances, last, info, low, q_buf, qs, state, pieces)
+    def back(units, trims, last, pieces, state):
+        return attend_back(heads, units, trims, last, info, low, q_buf, qs, state, pieces)
 
     up_1, state = after(up_1, state)
     up_2 = send(up_1, up)
     across_2 = send(up_1, [(i, i ^ 2) for i in devices])
-    state = back((2, 2), False, (up_1, swap(up_1)), state)
+    state = back(((2, 2),), (0,), False, (up_1, swap(up_1)), state)
     across_1, state = after(across_1, state)
-    state = back((0, 1), False, (across_1, swap(across_1, odd)), state)
+    state = back(((0, 1),), (0,), False, (across_1, swap(across_1, odd)), state)
     up_2, state = after(up_2, state)
     across_2, state = after(across_2, state)
     across_3 = send(up_2, [(i, i - 2) for i in odd])
-    up_2_other = swap(up_2)
-    across_2_other = swap(across_2)
-    state = back((4, 4), False, (up_2, up_2_other), state)
-    state = back((1, 3), False, (across_2, across_2_other), state)
+    pieces = (up_2, swap(up_2), across_2, swap(across_2))
+    state = back(((4, 4), (1, 3)), TRIMS, False, pieces, state)
     across_3, state = after(across_3, state)
-    out = back((3, 0), True, (across_3, swap(across_3, even)), state)
+    out = back(((3, 0),), TRIMS, True, (across_3, swap(across_3, even)), state)
     return out.reshape(tokens, heads, width)
 
 

time: 83.4 us -> 83.4 us (level)
  Pallas kernels: 32 us -> 29.6 us
  waiting for transfers between devices: 29.5 us -> 31.5 us
    pallas_call x5 -> x4, Pallas kernels: 24.3 us -> 22.3 us  [attend_back(): pl.pallas_call(functools.partial(back_kernel, heads, units, trims, last),...]
    ppermute x11, waiting for transfers between devices: 29.5 us -> 31.5 us  [send(): return lax.ppermute(x, AXES, pairs)]
  transfers between devices with their start and end apart: 11 -> 11, of which waited for: 6 -> 7; matrix products, arithmetic and copies ran while one was open for 0% -> 0% of each run, Pallas kernels for 32% -> 29%
where the time goes in v1:
time: 83.4 us; the launch traced here: 82.9 us
  waiting for transfers between devices  31.5 us (38%)
  Pallas kernels  29.6 us (35%)
  starting transfers between devices  20.5 us (25%)
  other arithmetic  1.05 us (1%)
    ppermute x11, waiting for transfers between devices, send(): return lax.ppermute(x, AXES, pairs)  31.5 us
    pallas_call x4, Pallas kernels, attend_back(): pl.pallas_call(functools.partial(back_kernel, heads, units, trims, last),...  22.3 us
    ppermute x11, starting transfers between devices, send(): return lax.ppermute(x, AXES, pairs)  20.5 us
    pallas_call x1, Pallas kernels, attend_own(): pl.pallas_call(functools.partial(own_kernel, heads), name='own_pair', out...  7.25 us
  transfers between devices with their start and end apart: 11, of which 7 were waited for; matrix products, arithmetic and copies ran while one was open for 0% of the time, Pallas kernels for 29%

profile of v1, /device:TPU:24, one launch (start us, length us, event | category | flops | bytes accessed | tf_op | source)
XLA Modules:
  0.0 82.9 jit_solution(13794208757153039914)
XLA Ops:
  0.0 1.0 %pad_maximum_fusion = f32[2,384,128]{2,1,0:T(8,128)S(1)} fusion(f32[1,384,128]{2,1,0:T(8,128)} %bitcast.12, f32[1,384,128]{2,1,0:T(8,128)} %bitcast.13), kind=kLoop, calls=%fused_computation | loop fusion | flops 98304 | bytes 786432 | tf_op jit(solution)/shard_map/stack | solution.py:275
  1.1 0.1 collective-permute-start
  1.2 3.8 %collective-permute-start.1 = (f32[768,128]{1,0:T(8,128)S(1)}, f32[768,128]{1,0:T(8,128)S(1)}, u32[]{:S(2)}, u32[]{:S(2)}) collective-permute-start(f32[768,128]{1,0:T(8,128)S(1)} %bitcast.8), channel_id=1, source_target_pairs={{0,4},{1,5},{2,6},{3,7},{4,8},{5,9},{6,10},{7,11},{8,12},{9,13},{1... | collective-permute-start | bytes 1179656 | tf_op jit(solution)/shard_map/ppermute | solution.py:265
  5.0 0.0 collective-permute-done.other_ref
  5.0 7.2 %own_pair.1 = (f32[3072,128]{1,0:T(8,128)S(1)}, f32[3072,128]{1,0:T(8,128)S(1)}, f32[3072,128]{1,0:T(8,128)S(1)}, bf16[3072,256]{1,0:T(8,128)(2,1)S(1)}, s32[3072,128]{1,0:T(8,128)S(1)}, /*index=5*/s32[2]{0:T(128)S(1)}) custom-call(s32[1]{0:T(128)} %bitcast.info, s32[1,256]{1,0:T(1,128)} %bitcast.14, f32[3072,128]{1,0:T(8,128)} %bitcast.11, ...), custom_call_target="tpu_custom_call" | custom-call | tf_op jit(solution)/shard_map/own_pair/pallas_call | solution.py:218
  12.3 6.6 %collective-permute-done.1.rest_0_ = f32[768,128]{1,0:T(8,128)S(1)} collective-permute-done((f32[768,128]{1,0:T(8,128)S(1)}, f32[768,128]{1,0:T(8,128)S(1)}, u32[]{:S(2)}, u32[]{:S(2)}) %collective-permute-start.1) | collective-permute-done | bytes 393248 | tf_op jit(solution)/shard_map/ppermute | solution.py:265
  18.9 0.0 collective-permute-start.4
  18.9 4.9 %collective-permute-start.3 = (f32[768,128]{1,0:T(8,128)S(1)}, f32[768,128]{1,0:T(8,128)S(1)}, u32[]{:S(2)}, u32[]{:S(2)}) collective-permute-start(f32[768,128]{1,0:T(8,128)S(1)} %bitcast.10), channel_id=1, source_target_pairs={{0,2},{1,3},{4,6},{5,7},{8,10},{9,11},{12,14},{13,15},{16,18},{17,... | collective-permute-start | bytes 1179656 | tf_op jit(solution)/shard_map/ppermute | solution.py:265
  23.8 0.0 collective-permute-done.4.rest_1_
  23.8 8.1 %shard_map.46 = (f32[3072,128]{1,0:T(8,128)S(1)}, f32[3072,128]{1,0:T(8,128)S(1)}, f32[3072,128]{1,0:T(8,128)S(1)}) custom-call(s32[1]{0:T(128)} %bitcast.info, s32[2]{0:T(128)S(1)} %get-tuple-element.40.low_ref, bf16[3072,256]{1,0:T(8,128)(2,1)S(1)} %get-tuple-element.41.q_buf, ...), custom_call_target="tpu_custom_call", output_to_operand_aliasing={{0}: (4, {}), {1}: (5, {}), {2}: (6, {})} | custom-call | tf_op jit(solution)/shard_map/pallas_call | solution.py:242
  31.9 0.9 %collective-permute-done.3.rest_0_ = f32[768,128]{1,0:T(8,128)S(1)} collective-permute-done((f32[768,128]{1,0:T(8,128)S(1)}, f32[768,128]{1,0:T(8,128)S(1)}, u32[]{:S(2)}, u32[]{:S(2)}) %collective-permute-start.3) | collective-permute-done | bytes 393248 | tf_op jit(solution)/shard_map/ppermute | solution.py:265
  32.8 0.7 collective-permute-start.5
  33.5 1.9 %collective-permute-start.2 = (f32[768,128]{1,0:T(8,128)S(1)}, f32[768,128]{1,0:T(8,128)S(1)}, u32[]{:S(2)}, u32[]{:S(2)}) collective-permute-start(f32[768,128]{1,0:T(8,128)S(1)} %collective-permute-done.1.rest_0_), channel_id=1, source_target_pairs={{0,4},{1,5},{2,6},{3,7},{4,8},{5,9},{6,10},{7,11},{8,12},{9,13},{1... | collective-permute-start | bytes 1179656 | tf_op jit(solution)/shard_map/ppermute | solution.py:265
  35.4 5.3 %collective-permute-start.7 = (f32[768,128]{1,0:T(8,128)S(1)}, f32[768,128]{1,0:T(8,128)S(1)}, u32[]{:S(2)}, u32[]{:S(2)}) collective-permute-start(f32[768,128]{1,0:T(8,128)S(1)} %collective-permute-done.1.rest_0_), channel_id=1, source_target_pairs={{0,2},{1,3},{2,0},{3,1},{4,6},{5,7},{6,4},{7,5},{8,10},{9,11},{10,... | collective-permute-start | bytes 1179656 | tf_op jit(solution)/shard_map/ppermute | solution.py:265
  40.7 0.0 collective-permute-done.5.rest_1_
  40.7 0.8 shard_map.47
  41.5 6.7 %collective-permute-done.2.rest_0_ = f32[768,128]{1,0:T(8,128)S(1)} collective-permute-done((f32[768,128]{1,0:T(8,128)S(1)}, f32[768,128]{1,0:T(8,128)S(1)}, u32[]{:S(2)}, u32[]{:S(2)}) %collective-permute-start.2) | collective-permute-done | bytes 393248 | tf_op jit(solution)/shard_map/ppermute | solution.py:265
  48.2 10.8 %collective-permute-done.7.rest_2_ = f32[768,128]{1,0:T(8,128)S(1)} collective-permute-done((f32[768,128]{1,0:T(8,128)S(1)}, f32[768,128]{1,0:T(8,128)S(1)}, u32[]{:S(2)}, u32[]{:S(2)}) %collective-permute-start.7) | collective-permute-done | bytes 393248 | tf_op jit(solution)/shard_map/ppermute | solution.py:265
  58.9 0.0 collective-permute-start.9
  58.9 0.5 collective-permute-start.8
  59.4 1.3 %collective-permute-start.6 = (f32[768,128]{1,0:T(8,128)S(1)}, f32[768,128]{1,0:T(8,128)S(1)}, u32[]{:S(2)}, u32[]{:S(2)}) collective-permute-start(f32[768,128]{1,0:T(8,128)S(1)} %collective-permute-done.2.rest_0_), channel_id=1, source_target_pairs={{2,0},{3,1},{6,4},{7,5},{10,8},{11,9},{14,12},{15,13},{18,16},{19,... | collective-permute-start | bytes 1179656 | tf_op jit(solution)/shard_map/ppermute | solution.py:265
  60.7 0.0 collective-permute-done.9.rest_3_
  60.7 0.5 collective-permute-done.8.rest_1_
  61.2 8.2 %shard_map.48 = (f32[3072,128]{1,0:T(8,128)S(1)}, f32[3072,128]{1,0:T(8,128)S(1)}, f32[3072,128]{1,0:T(8,128)S(1)}) custom-call(s32[1]{0:T(128)} %bitcast.info, s32[2]{0:T(128)S(1)} %get-tuple-element.40.low_ref, bf16[3072,256]{1,0:T(8,128)(2,1)S(1)} %get-tuple-element.41.q_buf, ...), custom_call_target="tpu_custom_call", output_to_operand_aliasing={{0}: (4, {}), {1}: (5, {}), {2}: (6, {})} | custom-call | tf_op jit(solution)/shard_map/pallas_call | solution.py:242
  69.5 4.4 %collective-permute-done.6.rest_0_ = f32[768,128]{1,0:T(8,128)S(1)} collective-permute-done((f32[768,128]{1,0:T(8,128)S(1)}, f32[768,128]{1,0:T(8,128)S(1)}, u32[]{:S(2)}, u32[]{:S(2)}) %collective-permute-start.6) | collective-permute-done | bytes 393248 | tf_op jit(solution)/shard_map/ppermute | solution.py:265
  73.9 1.9 %collective-permute-start.10 = (f32[768,128]{1,0:T(8,128)S(1)}, f32[768,128]{1,0:T(8,128)S(1)}, u32[]{:S(2)}, u32[]{:S(2)}) collective-permute-start(f32[768,128]{1,0:T(8,128)S(1)} %collective-permute-done.6.rest_0_), channel_id=1, source_target_pairs={{0,1},{1,0},{4,5},{5,4},{8,9},{9,8},{12,13},{13,12},{16,17},{17,16... | collective-permute-start | bytes 1179656 | tf_op jit(solution)/shard_map/ppermute | solution.py:265
  75.8 1.7 %collective-permute-done.10.rest_1_ = f32[768,128]{1,0:T(8,128)S(1)} collective-permute-done((f32[768,128]{1,0:T(8,128)S(1)}, f32[768,128]{1,0:T(8,128)S(1)}, u32[]{:S(2)}, u32[]{:S(2)}) %collective-permute-start.10) | collective-permute-done | bytes 393248 | tf_op jit(solution)/shard_map/ppermute | solution.py:265
  77.5 5.2 %shard_map.49 = f32[3072,128]{1,0:T(8,128)} custom-call(s32[1]{0:T(128)} %bitcast.info, s32[2]{0:T(128)S(1)} %get-tuple-element.40.low_ref, bf16[3072,256]{1,0:T(8,128)(2,1)S(1)} %get-tuple-element.41.q_buf, s32[3072,128]{1,0:T(8,128)S(1)} %get-tuple-element.42.qs_ref, f32[3072,128]{1,0:T(8,128)S(1)} %get-tuple-element.71.acc_in, ...), custom_call_target="tpu_custom_call" | custom-call | tf_op jit(solution)/shard_map/pallas_call | solution.py:242
Async XLA Ops:
  1.1 3.9 %collective-permute-start = (f32[768,128]{1,0:T(8,128)S(1)}, f32[768,128]{1,0:T(8,128)S(1)}, u32[]{:S(2)}, u32[]{:S(2)}) collective-permute-start(f32[768,128]{1,0:T(8,128)S(1)} %bitcast.7), channel_id=1, source_target_pairs={{0,1},{1,0},{2,3},{3,2},{4,5},{5,4},{6,7},{7,6},{8,9},{9,8},{10,11... | collective-permute-start | bytes 1179656 | tf_op jit(solution)/shard_map/ppermute | solution.py:265
  1.2 17.7 %collective-permute-start.1 = (f32[768,128]{1,0:T(8,128)S(1)}, f32[768,128]{1,0:T(8,128)S(1)}, u32[]{:S(2)}, u32[]{:S(2)}) collective-permute-start(f32[768,128]{1,0:T(8,128)S(1)} %bitcast.8), channel_id=1, source_target_pairs={{0,4},{1,5},{2,6},{3,7},{4,8},{5,9},{6,10},{7,11},{8,12},{9,13},{1... | collective-permute-start | bytes 1179656 | tf_op jit(solution)/shard_map/ppermute | solution.py:265
  18.9 5.0 %collective-permute-start.4 = (f32[768,128]{1,0:T(8,128)S(1)}, f32[768,128]{1,0:T(8,128)S(1)}, u32[]{:S(2)}, u32[]{:S(2)}) collective-permute-start(f32[768,128]{1,0:T(8,128)S(1)} %collective-permute-done.1.rest_0_), channel_id=1, source_target_pairs={{0,1},{1,0},{2,3},{3,2},{4,5},{5,4},{6,7},{7,6},{8,9},{9,8},{10,11... | collective-permute-start | bytes 1179656 | tf_op jit(solution)/shard_map/ppermute | solution.py:265
  18.9 14.0 %collective-permute-start.3 = (f32[768,128]{1,0:T(8,128)S(1)}, f32[768,128]{1,0:T(8,128)S(1)}, u32[]{:S(2)}, u32[]{:S(2)}) collective-permute-start(f32[768,128]{1,0:T(8,128)S(1)} %bitcast.10), channel_id=1, source_target_pairs={{0,2},{1,3},{4,6},{5,7},{8,10},{9,11},{12,14},{13,15},{16,18},{17,... | collective-permute-start | bytes 1179656 | tf_op jit(solution)/shard_map/ppermute | solution.py:265
  32.8 7.9 %collective-permute-start.5 = (f32[768,128]{1,0:T(8,128)S(1)}, f32[768,128]{1,0:T(8,128)S(1)}, u32[]{:S(2)}, u32[]{:S(2)}) collective-permute-start(f32[768,128]{1,0:T(8,128)S(1)} %collective-permute-done.3.rest_0_), channel_id=1, source_target_pairs={{2,3},{3,2},{6,7},{7,6},{10,11},{11,10},{14,15},{15,14},{18,19},{1... | collective-permute-start | bytes 1179656 | tf_op jit(solution)/shard_map/ppermute | solution.py:265
  33.5 14.7 %collective-permute-start.2 = (f32[768,128]{1,0:T(8,128)S(1)}, f32[768,128]{1,0:T(8,128)S(1)}, u32[]{:S(2)}, u32[]{:S(2)}) collective-permute-start(f32[768,128]{1,0:T(8,128)S(1)} %collective-permute-done.1.rest_0_), channel_id=1, source_target_pairs={{0,4},{1,5},{2,6},{3,7},{4,8},{5,9},{6,10},{7,11},{8,12},{9,13},{1... | collective-permute-start | bytes 1179656 | tf_op jit(solution)/shard_map/ppermute | solution.py:265
  35.4 23.5 %collective-permute-start.7 = (f32[768,128]{1,0:T(8,128)S(1)}, f32[768,128]{1,0:T(8,128)S(1)}, u32[]{:S(2)}, u32[]{:S(2)}) collective-permute-start(f32[768,128]{1,0:T(8,128)S(1)} %collective-permute-done.1.rest_0_), channel_id=1, source_target_pairs={{0,2},{1,3},{2,0},{3,1},{4,6},{5,7},{6,4},{7,5},{8,10},{9,11},{10,... | collective-permute-start | bytes 1179656 | tf_op jit(solution)/shard_map/ppermute | solution.py:265
  58.9 1.8 %collective-permute-start.9 = (f32[768,128]{1,0:T(8,128)S(1)}, f32[768,128]{1,0:T(8,128)S(1)}, u32[]{:S(2)}, u32[]{:S(2)}) collective-permute-start(f32[768,128]{1,0:T(8,128)S(1)} %collective-permute-done.7.rest_2_), channel_id=1, source_target_pairs={{0,1},{1,0},{2,3},{3,2},{4,5},{5,4},{6,7},{7,6},{8,9},{9,8},{10,11... | collective-permute-start | bytes 1179656 | tf_op jit(solution)/shard_map/ppermute | solution.py:265
  58.9 2.3 %collective-permute-start.8 = (f32[768,128]{1,0:T(8,128)S(1)}, f32[768,128]{1,0:T(8,128)S(1)}, u32[]{:S(2)}, u32[]{:S(2)}) collective-permute-start(f32[768,128]{1,0:T(8,128)S(1)} %collective-permute-done.2.rest_0_), channel_id=1, source_target_pairs={{0,1},{1,0},{2,3},{3,2},{4,5},{5,4},{6,7},{7,6},{8,9},{9,8},{10,11... | collective-permute-start | bytes 1179656 | tf_op jit(solution)/shard_map/ppermute | solution.py:265
  59.4 14.4 %collective-permute-start.6 = (f32[768,128]{1,0:T(8,128)S(1)}, f32[768,128]{1,0:T(8,128)S(1)}, u32[]{:S(2)}, u32[]{:S(2)}) collective-permute-start(f32[768,128]{1,0:T(8,128)S(1)} %collective-permute-done.2.rest_0_), channel_id=1, source_target_pairs={{2,0},{3,1},{6,4},{7,5},{10,8},{11,9},{14,12},{15,13},{18,16},{19,... | collective-permute-start | bytes 1179656 | tf_op jit(solution)/shard_map/ppermute | solution.py:265
  73.9 3.6 %collective-permute-start.10 = (f32[768,128]{1,0:T(8,128)S(1)}, f32[768,128]{1,0:T(8,128)S(1)}, u32[]{:S(2)}, u32[]{:S(2)}) collective-permute-start(f32[768,128]{1,0:T(8,128)S(1)} %collective-permute-done.6.rest_0_), channel_id=1, source_target_pairs={{0,1},{1,0},{4,5},{5,4},{8,9},{9,8},{12,13},{13,12},{16,17},{17,16... | collective-permute-start | bytes 1179656 | tf_op jit(solution)/shard_map/ppermute | solution.py:265

commit v2 on v1

--- a/solution.py
+++ b/solution.py
@@ -284,13 +284,16 @@
     up_1, state = after(up_1, state)
     up_2 = send(up_1, up)
     across_2 = send(up_1, [(i, i ^ 2) for i in devices])
-    state = back(((2, 2),), (0,), False, (up_1, swap(up_1)), state)
+    up_1_other = swap(up_1)
     across_1, state = after(across_1, state)
-    state = back(((0, 1),), (0,), False, (across_1, swap(across_1, odd)), state)
+    across_1_other = swap(across_1, odd)
+    state = back(((2, 2),), (0,), False, (up_1, up_1_other), state)
     up_2, state = after(up_2, state)
+    across_3 = send(up_2, [(i, i - 2) for i in odd])
+    up_2_other = swap(up_2)
+    state = back(((0, 1),), (0,), False, (across_1, across_1_other), state)
     across_2, state = after(across_2, state)
-    across_3 = send(up_2, [(i, i - 2) for i in odd])
-    pieces = (up_2, swap(up_2), across_2, swap(across_2))
+    pieces = (up_2, up_2_other, across_2, swap(across_2))
     state = back(((4, 4), (1, 3)), TRIMS, False, pieces, state)
     across_3, state = after(across_3, state)
     out = back(((3, 0),), TRIMS, True, (across_3, swap(across_3, even)), state)

time: 83.4 us -> 71.8 us (0.86)
  waiting for transfers between devices: 31.5 us -> 17.3 us
  starting transfers between devices: 20.5 us -> 23 us
    ppermute x11, waiting for transfers between devices: 31.5 us -> 17.3 us  [send(): return lax.ppermute(x, AXES, pairs)]
    ppermute x11, starting transfers between devices: 20.5 us -> 23 us  [send(): return lax.ppermute(x, AXES, pairs)]
  transfers between devices with their start and end apart: 11 -> 11, of which waited for: 7 -> 6; matrix products, arithmetic and copies ran while one was open for 0% -> 0% of each run, Pallas kernels for 29% -> 34%
where the time goes in v2:
time: 71.8 us; the launch traced here: 71.2 us
  Pallas kernels  29.6 us (41%)
  starting transfers between devices  23 us (32%)
  waiting for transfers between devices  17.3 us (24%)
  other arithmetic  1.05 us (1%)
    ppermute x11, starting transfers between devices, send(): return lax.ppermute(x, AXES, pairs)  23 us
    pallas_call x4, Pallas kernels, attend_back(): pl.pallas_call(functools.partial(back_kernel, heads, units, trims, last),...  22.3 us
    ppermute x11, waiting for transfers between devices, send(): return lax.ppermute(x, AXES, pairs)  17.3 us
    pallas_call x1, Pallas kernels, attend_own(): pl.pallas_call(functools.partial(own_kernel, heads), name='own_pair', out...  7.25 us
  transfers between devices with their start and end apart: 11, of which 6 were waited for; matrix products, arithmetic and copies ran while one was open for 0% of the time, Pallas kernels for 34%

profile of v2, /device:TPU:24, one launch (start us, length us, event | category | flops | bytes accessed | tf_op | source)
XLA Modules:
  0.0 71.2 jit_solution(6526350858082987602)
XLA Ops:
  0.0 1.0 %pad_maximum_fusion = f32[2,384,128]{2,1,0:T(8,128)S(1)} fusion(f32[1,384,128]{2,1,0:T(8,128)} %bitcast.12, f32[1,384,128]{2,1,0:T(8,128)} %bitcast.13), kind=kLoop, calls=%fused_computation | loop fusion | flops 98304 | bytes 786432 | tf_op jit(solution)/shard_map/stack | solution.py:275
  1.1 0.1 collective-permute-start
  1.2 3.8 %collective-permute-start.1 = (f32[768,128]{1,0:T(8,128)S(1)}, f32[768,128]{1,0:T(8,128)S(1)}, u32[]{:S(2)}, u32[]{:S(2)}) collective-permute-start(f32[768,128]{1,0:T(8,128)S(1)} %bitcast.8), channel_id=1, source_target_pairs={{0,4},{1,5},{2,6},{3,7},{4,8},{5,9},{6,10},{7,11},{8,12},{9,13},{1... | collective-permute-start | bytes 1179656 | tf_op jit(solution)/shard_map/ppermute | solution.py:265
  5.0 5.0 %collective-permute-start.3 = (f32[768,128]{1,0:T(8,128)S(1)}, f32[768,128]{1,0:T(8,128)S(1)}, u32[]{:S(2)}, u32[]{:S(2)}) collective-permute-start(f32[768,128]{1,0:T(8,128)S(1)} %bitcast.9), channel_id=1, source_target_pairs={{0,2},{1,3},{4,6},{5,7},{8,10},{9,11},{12,14},{13,15},{16,18},{17,... | collective-permute-start | bytes 1179656 | tf_op jit(solution)/shard_map/ppermute | solution.py:265
  10.0 0.0 collective-permute-done.other_ref
  10.0 7.3 %own_pair.1 = (f32[3072,128]{1,0:T(8,128)S(1)}, f32[3072,128]{1,0:T(8,128)S(1)}, f32[3072,128]{1,0:T(8,128)S(1)}, bf16[3072,256]{1,0:T(8,128)(2,1)S(1)}, s32[3072,128]{1,0:T(8,128)S(1)}, /*index=5*/s32[2]{0:T(128)S(1)}) custom-call(s32[1]{0:T(128)} %bitcast.info, s32[1,256]{1,0:T(1,128)} %bitcast.14, f32[3072,128]{1,0:T(8,128)} %bitcast.11, ...), custom_call_target="tpu_custom_call" | custom-call | tf_op jit(solution)/shard_map/own_pair/pallas_call | solution.py:218
  17.2 1.6 %collective-permute-done.1.rest_0_ = f32[768,128]{1,0:T(8,128)S(1)} collective-permute-done((f32[768,128]{1,0:T(8,128)S(1)}, f32[768,128]{1,0:T(8,128)S(1)}, u32[]{:S(2)}, u32[]{:S(2)}) %collective-permute-start.1) | collective-permute-done | bytes 393248 | tf_op jit(solution)/shard_map/ppermute | solution.py:265
  18.9 0.6 collective-permute-start.4
  19.4 3.8 %collective-permute-start.2 = (f32[768,128]{1,0:T(8,128)S(1)}, f32[768,128]{1,0:T(8,128)S(1)}, u32[]{:S(2)}, u32[]{:S(2)}) collective-permute-start(f32[768,128]{1,0:T(8,128)S(1)} %collective-permute-done.1.rest_0_), channel_id=1, source_target_pairs={{0,4},{1,5},{2,6},{3,7},{4,8},{5,9},{6,10},{7,11},{8,12},{9,13},{1... | collective-permute-start | bytes 1179656 | tf_op jit(solution)/shard_map/ppermute | solution.py:265
  23.2 2.8 %collective-permute-done.3.rest_0_ = f32[768,128]{1,0:T(8,128)S(1)} collective-permute-done((f32[768,128]{1,0:T(8,128)S(1)}, f32[768,128]{1,0:T(8,128)S(1)}, u32[]{:S(2)}, u32[]{:S(2)}) %collective-permute-start.3) | collective-permute-done | bytes 393248 | tf_op jit(solution)/shard_map/ppermute | solution.py:265
  26.1 0.7 collective-permute-start.7
  26.8 5.3 %collective-permute-start.6 = (f32[768,128]{1,0:T(8,128)S(1)}, f32[768,128]{1,0:T(8,128)S(1)}, u32[]{:S(2)}, u32[]{:S(2)}) collective-permute-start(f32[768,128]{1,0:T(8,128)S(1)} %collective-permute-done.1.rest_0_), channel_id=1, source_target_pairs={{0,2},{1,3},{2,0},{3,1},{4,6},{5,7},{6,4},{7,5},{8,10},{9,11},{10,... | collective-permute-start | bytes 1179656 | tf_op jit(solution)/shard_map/ppermute | solution.py:265
  32.1 0.0 collective-permute-done.4.rest_1_
  32.1 8.1 %shard_map.46 = (f32[3072,128]{1,0:T(8,128)S(1)}, f32[3072,128]{1,0:T(8,128)S(1)}, f32[3072,128]{1,0:T(8,128)S(1)}) custom-call(s32[1]{0:T(128)} %bitcast.info, s32[2]{0:T(128)S(1)} %get-tuple-element.40.low_ref, bf16[3072,256]{1,0:T(8,128)(2,1)S(1)} %get-tuple-element.41.q_buf, ...), custom_call_target="tpu_custom_call", output_to_operand_aliasing={{0}: (4, {}), {1}: (5, {}), {2}: (6, {})} | custom-call | tf_op jit(solution)/shard_map/pallas_call | solution.py:242
  40.2 0.0 collective-permute-done.2.rest_0_
  40.2 0.0 collective-permute-done.7.rest_1_
  40.2 0.8 %shard_map.47 = (f32[3072,128]{1,0:T(8,128)S(1)}, f32[3072,128]{1,0:T(8,128)S(1)}, f32[3072,128]{1,0:T(8,128)S(1)}) custom-call(s32[1]{0:T(128)} %bitcast.info, s32[2]{0:T(128)S(1)} %get-tuple-element.40.low_ref, bf16[3072,256]{1,0:T(8,128)(2,1)S(1)} %get-tuple-element.41.q_buf, ...), custom_call_target="tpu_custom_call", output_to_operand_aliasing={{0}: (4, {}), {1}: (5, {}), {2}: (6, {})} | custom-call | tf_op jit(solution)/shard_map/pallas_call | solution.py:242
  41.0 6.2 %collective-permute-done.6.rest_2_ = f32[768,128]{1,0:T(8,128)S(1)} collective-permute-done((f32[768,128]{1,0:T(8,128)S(1)}, f32[768,128]{1,0:T(8,128)S(1)}, u32[]{:S(2)}, u32[]{:S(2)}) %collective-permute-start.6) | collective-permute-done | bytes 393248 | tf_op jit(solution)/shard_map/ppermute | solution.py:265
  47.2 0.1 collective-permute-start.9
  47.3 0.4 collective-permute-start.8
  47.7 1.3 %collective-permute-start.5 = (f32[768,128]{1,0:T(8,128)S(1)}, f32[768,128]{1,0:T(8,128)S(1)}, u32[]{:S(2)}, u32[]{:S(2)}) collective-permute-start(f32[768,128]{1,0:T(8,128)S(1)} %collective-permute-done.2.rest_0_), channel_id=1, source_target_pairs={{2,0},{3,1},{6,4},{7,5},{10,8},{11,9},{14,12},{15,13},{18,16},{19,... | collective-permute-start | bytes 1179656 | tf_op jit(solution)/shard_map/ppermute | solution.py:265
  49.0 0.0 collective-permute-done.9.rest_3_
  49.0 0.5 collective-permute-done.8.rest_1_
  49.5 8.2 %shard_map.48 = (f32[3072,128]{1,0:T(8,128)S(1)}, f32[3072,128]{1,0:T(8,128)S(1)}, f32[3072,128]{1,0:T(8,128)S(1)}) custom-call(s32[1]{0:T(128)} %bitcast.info, s32[2]{0:T(128)S(1)} %get-tuple-element.40.low_ref, bf16[3072,256]{1,0:T(8,128)(2,1)S(1)} %get-tuple-element.41.q_buf, ...), custom_call_target="tpu_custom_call", output_to_operand_aliasing={{0}: (4, {}), {1}: (5, {}), {2}: (6, {})} | custom-call | tf_op jit(solution)/shard_map/pallas_call | solution.py:242
  57.7 4.5 %collective-permute-done.5.rest_0_ = f32[768,128]{1,0:T(8,128)S(1)} collective-permute-done((f32[768,128]{1,0:T(8,128)S(1)}, f32[768,128]{1,0:T(8,128)S(1)}, u32[]{:S(2)}, u32[]{:S(2)}) %collective-permute-start.5) | collective-permute-done | bytes 393248 | tf_op jit(solution)/shard_map/ppermute | solution.py:265
  62.2 1.9 %collective-permute-start.10 = (f32[768,128]{1,0:T(8,128)S(1)}, f32[768,128]{1,0:T(8,128)S(1)}, u32[]{:S(2)}, u32[]{:S(2)}) collective-permute-start(f32[768,128]{1,0:T(8,128)S(1)} %collective-permute-done.5.rest_0_), channel_id=1, source_target_pairs={{0,1},{1,0},{4,5},{5,4},{8,9},{9,8},{12,13},{13,12},{16,17},{17,16... | collective-permute-start | bytes 1179656 | tf_op jit(solution)/shard_map/ppermute | solution.py:265
  64.1 1.7 %collective-permute-done.10.rest_1_ = f32[768,128]{1,0:T(8,128)S(1)} collective-permute-done((f32[768,128]{1,0:T(8,128)S(1)}, f32[768,128]{1,0:T(8,128)S(1)}, u32[]{:S(2)}, u32[]{:S(2)}) %collective-permute-start.10) | collective-permute-done | bytes 393248 | tf_op jit(solution)/shard_map/ppermute | solution.py:265
  65.8 5.2 %shard_map.49 = f32[3072,128]{1,0:T(8,128)} custom-call(s32[1]{0:T(128)} %bitcast.info, s32[2]{0:T(128)S(1)} %get-tuple-element.40.low_ref, bf16[3072,256]{1,0:T(8,128)(2,1)S(1)} %get-tuple-element.41.q_buf, s32[3072,128]{1,0:T(8,128)S(1)} %get-tuple-element.42.qs_ref, f32[3072,128]{1,0:T(8,128)S(1)} %get-tuple-element.71.acc_in, ...), custom_call_target="tpu_custom_call" | custom-call | tf_op jit(solution)/shard_map/pallas_call | solution.py:242
Async XLA Ops:
  1.1 8.9 %collective-permute-start = (f32[768,128]{1,0:T(8,128)S(1)}, f32[768,128]{1,0:T(8,128)S(1)}, u32[]{:S(2)}, u32[]{:S(2)}) collective-permute-start(f32[768,128]{1,0:T(8,128)S(1)} %bitcast.7), channel_id=1, source_target_pairs={{0,1},{1,0},{2,3},{3,2},{4,5},{5,4},{6,7},{7,6},{8,9},{9,8},{10,11... | collective-permute-start | bytes 1179656 | tf_op jit(solution)/shard_map/ppermute | solution.py:265
  1.2 17.7 %collective-permute-start.1 = (f32[768,128]{1,0:T(8,128)S(1)}, f32[768,128]{1,0:T(8,128)S(1)}, u32[]{:S(2)}, u32[]{:S(2)}) collective-permute-start(f32[768,128]{1,0:T(8,128)S(1)} %bitcast.8), channel_id=1, source_target_pairs={{0,4},{1,5},{2,6},{3,7},{4,8},{5,9},{6,10},{7,11},{8,12},{9,13},{1... | collective-permute-start | bytes 1179656 | tf_op jit(solution)/shard_map/ppermute | solution.py:265
  5.0 21.1 %collective-permute-start.3 = (f32[768,128]{1,0:T(8,128)S(1)}, f32[768,128]{1,0:T(8,128)S(1)}, u32[]{:S(2)}, u32[]{:S(2)}) collective-permute-start(f32[768,128]{1,0:T(8,128)S(1)} %bitcast.9), channel_id=1, source_target_pairs={{0,2},{1,3},{4,6},{5,7},{8,10},{9,11},{12,14},{13,15},{16,18},{17,... | collective-permute-start | bytes 1179656 | tf_op jit(solution)/shard_map/ppermute | solution.py:265
  18.9 13.3 %collective-permute-start.4 = (f32[768,128]{1,0:T(8,128)S(1)}, f32[768,128]{1,0:T(8,128)S(1)}, u32[]{:S(2)}, u32[]{:S(2)}) collective-permute-start(f32[768,128]{1,0:T(8,128)S(1)} %collective-permute-done.1.rest_0_), channel_id=1, source_target_pairs={{0,1},{1,0},{2,3},{3,2},{4,5},{5,4},{6,7},{7,6},{8,9},{9,8},{10,11... | collective-permute-start | bytes 1179656 | tf_op jit(solution)/shard_map/ppermute | solution.py:265
  19.4 20.8 %collective-permute-start.2 = (f32[768,128]{1,0:T(8,128)S(1)}, f32[768,128]{1,0:T(8,128)S(1)}, u32[]{:S(2)}, u32[]{:S(2)}) collective-permute-start(f32[768,128]{1,0:T(8,128)S(1)} %collective-permute-done.1.rest_0_), channel_id=1, source_target_pairs={{0,4},{1,5},{2,6},{3,7},{4,8},{5,9},{6,10},{7,11},{8,12},{9,13},{1... | collective-permute-start | bytes 1179656 | tf_op jit(solution)/shard_map/ppermute | solution.py:265
  26.1 14.1 %collective-permute-start.7 = (f32[768,128]{1,0:T(8,128)S(1)}, f32[768,128]{1,0:T(8,128)S(1)}, u32[]{:S(2)}, u32[]{:S(2)}) collective-permute-start(f32[768,128]{1,0:T(8,128)S(1)} %collective-permute-done.3.rest_0_), channel_id=1, source_target_pairs={{2,3},{3,2},{6,7},{7,6},{10,11},{11,10},{14,15},{15,14},{18,19},{1... | collective-permute-start | bytes 1179656 | tf_op jit(solution)/shard_map/ppermute | solution.py:265
  26.8 20.4 %collective-permute-start.6 = (f32[768,128]{1,0:T(8,128)S(1)}, f32[768,128]{1,0:T(8,128)S(1)}, u32[]{:S(2)}, u32[]{:S(2)}) collective-permute-start(f32[768,128]{1,0:T(8,128)S(1)} %collective-permute-done.1.rest_0_), channel_id=1, source_target_pairs={{0,2},{1,3},{2,0},{3,1},{4,6},{5,7},{6,4},{7,5},{8,10},{9,11},{10,... | collective-permute-start | bytes 1179656 | tf_op jit(solution)/shard_map/ppermute | solution.py:265
  47.2 1.8 %collective-permute-start.9 = (f32[768,128]{1,0:T(8,128)S(1)}, f32[768,128]{1,0:T(8,128)S(1)}, u32[]{:S(2)}, u32[]{:S(2)}) collective-permute-start(f32[768,128]{1,0:T(8,128)S(1)} %collective-permute-done.6.rest_2_), channel_id=1, source_target_pairs={{0,1},{1,0},{2,3},{3,2},{4,5},{5,4},{6,7},{7,6},{8,9},{9,8},{10,11... | collective-permute-start | bytes 1179656 | tf_op jit(solution)/shard_map/ppermute | solution.py:265
  47.3 2.2 %collective-permute-start.8 = (f32[768,128]{1,0:T(8,128)S(1)}, f32[768,128]{1,0:T(8,128)S(1)}, u32[]{:S(2)}, u32[]{:S(2)}) collective-permute-start(f32[768,128]{1,0:T(8,128)S(1)} %collective-permute-done.2.rest_0_), channel_id=1, source_target_pairs={{0,1},{1,0},{2,3},{3,2},{4,5},{5,4},{6,7},{7,6},{8,9},{9,8},{10,11... | collective-permute-start | bytes 1179656 | tf_op jit(solution)/shard_map/ppermute | solution.py:265
  47.7 14.5 %collective-permute-start.5 = (f32[768,128]{1,0:T(8,128)S(1)}, f32[768,128]{1,0:T(8,128)S(1)}, u32[]{:S(2)}, u32[]{:S(2)}) collective-permute-start(f32[768,128]{1,0:T(8,128)S(1)} %collective-permute-done.2.rest_0_), channel_id=1, source_target_pairs={{2,0},{3,1},{6,4},{7,5},{10,8},{11,9},{14,12},{15,13},{18,16},{19,... | collective-permute-start | bytes 1179656 | tf_op jit(solution)/shard_map/ppermute | solution.py:265
  62.2 3.6 %collective-permute-start.10 = (f32[768,128]{1,0:T(8,128)S(1)}, f32[768,128]{1,0:T(8,128)S(1)}, u32[]{:S(2)}, u32[]{:S(2)}) collective-permute-start(f32[768,128]{1,0:T(8,128)S(1)} %collective-permute-done.5.rest_0_), channel_id=1, source_target_pairs={{0,1},{1,0},{4,5},{5,4},{8,9},{9,8},{12,13},{13,12},{16,17},{17,16... | collective-permute-start | bytes 1179656 | tf_op jit(solution)/shard_map/ppermute | solution.py:265
